TPU v7x, 128 devices: a whole 4x4x4 slice. The times are simulated.
128 devices in a mesh: dp: 16 (over y_hi, z, core), tensor: 8 (over x, y_lo).
Axes of the slice: x: 4, y: 4 (y_hi: 2, y_lo: 2; y = y_hi * 2 + y_lo), z: 4, core: 2. Of those that a mesh axis runs over, the one named last changes fastest.
Arguments:
- activations: bfloat16 [16384, 8192], P('dp'), may hold values from -6 to 6
- out_grad: bfloat16 [16384, 28672], P('dp', 'tensor'), may hold values from -0.046875 to 0.046875
- projector: bfloat16 [8192, 512], P(('dp', 'tensor')), may hold values from -0.0625 to 0.0625
- first_moment: float32 [512, 28672], P('dp', 'tensor'), may hold values from -3 to 3
- second_moment: float32 [512, 28672], P('dp', 'tensor'), may hold values from 0.1 to 4
Outputs:
- update: float32 [8192, 28672], P('dp', 'tensor')
- new_first: float32 [512, 28672], P('dp', 'tensor')
- new_second: float32 [512, 28672], P('dp', 'tensor')
All inputs are finite; a program needn't handle non-finite values.
Results may differ from a plain program's by a relative error of at most 0.0031.
Values may be sent and summed in bfloat16 or wider, within the bound.
A program may use at most 128 MiB of HBM per device.

v0:
```python
import jax
import jax.numpy as jnp
from jax import lax
from jax.sharding import PartitionSpec as P

beta_one = 0.9
beta_two = 0.999
bias_one = 1.0 - 0.9**10
bias_two = 1.0 - 0.999**10
adam_eps = 1e-08


def in_order(tiles, dim):
    dims = list(tiles.shape[1:])
    dims[dim] *= tiles.shape[0]
    return jnp.moveaxis(tiles, 0, dim).reshape(dims)


def sent_to_all(shard, axis):
    copies = jnp.broadcast_to(shard, (lax.axis_size(axis), *shard.shape))
    return lax.all_to_all(copies, axis, split_axis=0, concat_axis=0, tiled=True)


def collect(shard, axis, dim):
    return in_order(sent_to_all(shard, axis), dim)


def per_device(activations, out_grad, projector, first_moment, second_moment):
    token_rows = activations.shape[0]
    lane_blocks = collect(projector, "dp", 0)
    data_lanes = lax.axis_size("dp")
    tensor_lanes = lax.axis_size("tensor")
    block_rows = projector.shape[0]
    split_cols = activations.reshape(token_rows, data_lanes, tensor_lanes, block_rows)
    chosen = lax.dynamic_index_in_dim(split_cols, lax.axis_index("tensor"), 2, keepdims=False)
    chosen = chosen.reshape(token_rows, data_lanes * block_rows)
    partial_sum = jnp.dot(chosen, lane_blocks, preferred_element_type=jnp.float32)
    projected = lax.psum(partial_sum, "tensor")
    projected = projected.astype(jnp.bfloat16)
    coefficients = lax.psum_scatter(
        lax.dot_general(
            projected, out_grad, (((0,), (0,)), ((), ())), preferred_element_type=jnp.float32
        ),
        "dp",
        scatter_dimension=0,
        tiled=True,
    )
    new_first = beta_one * first_moment + (1.0 - beta_one) * coefficients
    new_second = beta_two * second_moment + (1.0 - beta_two) * coefficients * coefficients
    normalized = (new_first / bias_one / (jnp.sqrt(new_second / bias_two) + adam_eps)).astype(
        jnp.bfloat16
    )
    basis_rows = collect(projector, "tensor", 0)
    update = jnp.dot(
        basis_rows,
        lax.all_gather(normalized, "dp", axis=0, tiled=True),
        preferred_element_type=jnp.float32,
    )
    return (update, new_first, new_second)


def solution(mesh):
    in_specs = (
        P("dp", None),
        P("dp", "tensor"),
        P(("dp", "tensor"), None),
        P("dp", "tensor"),
        P("dp", "tensor"),
    )
    out_specs = (P("dp", "tensor"), P("dp", "tensor"), P("dp", "tensor"))
    return jax.shard_map(
        per_device, mesh=mesh, in_specs=in_specs, out_specs=out_specs, check_vma=False
    )
```

profile of v0, /device:TPU:1, one launch (start us, length us, event | category | flops | bytes accessed | tf_op | source)
XLA Modules:
  0.0 319.9 jit_solution(16738832030383836894)
XLA Ops:
  7.2 1.9 broadcast_in_dim.6
  9.1 9.4 %all-to-all-start = ((bf16[16,64,512]{2,1,0:T(8,128)(2,1)}), bf16[16,64,512]{2,1,0:T(8,128)(2,1)S(1)}, u32[]{:S(2)}, u32[]{:S(2)}) async-start(bf16[16,64,512]{2,1,0:T(8,128)(2,1)} %broadcast_in_dim.6), calls=%async_computation | async-start | bytes 2097152 | tf_op jit(solution)/shard_map/all_to_all | solution.py:21
  18.5 0.0 reduce-scatter.2.cloned.1.call-start
  18.6 22.4 %copy.9 = bf16[1024,8192]{0,1:T(8,128)(2,1)} copy(bf16[1024,8192]{1,0:T(8,128)(2,1)} %param.5) | data formatting | bytes 33554432 | tf_op args[0]
  41.0 3.1 constant_dynamic-slice_fusion
  44.2 0.0 all-to-all-done
  44.2 2.9 fusion.4
  47.0 84.2 %all-reduce.1 = bf16[1024,512]{1,0:T(8,128)(2,1)S(1)} all-reduce(f32[1024,512]{1,0:T(8,128)S(1)} %fusion.4), channel_id=1, replica_groups=mesh['dp'=16,'tensor'=8] {'tensor'}, use_global_device_ids=true, to_apply=%region_0.1 | all-reduce | flops 524288 | bytes 3145728 | tf_op jit(solution)/shard_map/psum | solution.py:38
  131.3 9.2 %fusion.5 = f32[512,3584]{1,0:T(8,128)} fusion(bf16[1024,512]{1,0:T(8,128)(2,1)S(1)} %all-reduce.1, bf16[1024,3584]{1,0:T(8,128)(2,1)} %param.6), kind=kOutput, calls=%fused_computation.9 | convolution fusion | flops 3758096384 | bytes 15728640 | tf_op jit(solution)/shard_map/dot_general | solution.py:41
  140.4 0.0 copy-start
  140.4 0.0 copy-start.1
  140.4 0.0 copy-start.2
  140.4 0.0 reduce-scatter.2.cloned.1.call-update
  140.5 0.0 all-gather.2.cloned.1.call-start
  140.5 100.7 %reduce-scatter.2.cloned.1.call-done = f32[32,3584]{1,0:T(8,128)} async-done(((f32[512,3584]{1,0:T(8,128)}), f32[32,3584]{1,0:T(8,128)}) %reduce-scatter.2.cloned.1.call-update) | async-done | bytes 458768 | tf_op jit(solution)/shard_map/reduce_scatter | solution.py:40
  241.2 0.0 copy-done
  241.2 0.0 copy-done.1
  241.2 2.2 divide_convert_fusion
  243.4 0.0 all-gather.2.cloned.1.call-update
  243.4 0.0 copy-done.2
  243.5 11.2 %all_to_all.10 = bf16[8,64,512]{2,1,0:T(8,128)(2,1)S(1)} all-to-all(bf16[8,64,512]{2,1,0:T(8,128)(2,1)S(1)} %broadcast_in_dim.7), channel_id=1, replica_groups=mesh['dp'=16,'tensor'=8] {'tensor'}, dimensions={0} | all-to-all | bytes 1048576 | tf_op jit(solution)/shard_map/all_to_all | solution.py:21
  254.7 42.9 %all-gather.2.cloned.1.call-done = bf16[512,3584]{1,0:T(8,128)(2,1)} async-done(((bf16[32,3584]{1,0:T(8,128)(2,1)}), bf16[512,3584]{1,0:T(8,128)(2,1)}) %all-gather.2.cloned.1.call-update) | async-done | bytes 3670032 | tf_op jit(solution)/shard_map/all_gather | solution.py:56
  297.6 7.1 %convolution_bitcast_fusion = f32[512,3584]{0,1:T(8,128)} fusion(bf16[512,3584]{1,0:T(8,128)(2,1)} %all-gather.2.cloned.1.call-done, bf16[512,512]{1,0:T(8,128)(2,1)S(1)} %bitcast.13), kind=kOutput, calls=%fused_computation | convolution fusion | flops 1879048192 | bytes 11534336 | tf_op jit(solution)/shard_map/dot_general | solution.py:54
  304.7 8.4 %copy.10 = f32[512,3584]{1,0:T(8,128)} copy(f32[512,3584]{0,1:T(8,128)} %convolution_bitcast_fusion) | data formatting | bytes 14680064
  (1 shorter events, 0.0 us)
Async XLA Ops:
  9.1 35.1 %all-to-all-start = ((bf16[16,64,512]{2,1,0:T(8,128)(2,1)}), bf16[16,64,512]{2,1,0:T(8,128)(2,1)S(1)}, u32[]{:S(2)}, u32[]{:S(2)}) async-start(bf16[16,64,512]{2,1,0:T(8,128)(2,1)} %broadcast_in_dim.6), calls=%async_computation | async-start | bytes 2097152 | tf_op jit(solution)/shard_map/all_to_all | solution.py:21
  18.5 222.7 %reduce-scatter.2.cloned.1.call-start = ((), (), s32[]{:S(2)}) async-start(), calls=%async_computation.3 | async-start | bytes 7798784 | tf_op jit(solution)/shard_map/reduce_scatter | solution.py:40
  140.4 100.8 %copy-start = (f32[32,3584]{1,0:T(8,128)S(1)}, f32[32,3584]{1,0:T(8,128)}, u32[]{:S(2)}) copy-start(f32[32,3584]{1,0:T(8,128)} %param.8) | copy-start | bytes 1376260
  140.4 100.8 %copy-start.1 = (f32[32,3584]{1,0:T(8,128)S(1)}, f32[32,3584]{1,0:T(8,128)}, u32[]{:S(2)}) copy-start(f32[32,3584]{1,0:T(8,128)} %param.9) | copy-start | bytes 1376260
  140.4 103.0 %copy-start.2 = (bf16[64,512]{1,0:T(8,128)(2,1)S(1)}, bf16[64,512]{1,0:T(8,128)(2,1)}, u32[]{:S(2)}) copy-start(bf16[64,512]{1,0:T(8,128)(2,1)} %param.7) | copy-start | bytes 196612
  140.5 157.1 %all-gather.2.cloned.1.call-start = ((), (), s32[]{:S(2)}) async-start(), calls=%async_computation.4 | async-start | bytes 3899392 | tf_op jit(solution)/shard_map/all_gather | solution.py:56
Sparse Core Ops, SparseCore 0:
  140.6 100.6 reduce-scatter.1
  244.3 53.2 all-gather.1
where the time goes:
time: 321 us; the launch traced here: 320 us
  waiting for transfers between devices  144 us (45%)
  blocking collectives  95.4 us (30%)
  local copies, waits for them, and re-layouts  35.9 us (11%)
  matrix products  19.1 us (6%)
  between operations  14.1 us (4%)
  starting transfers between devices  9.53 us (3%)
    reduce_scatter x1, waiting for transfers between devices, per_device(): lax.psum_scatter(lax.dot_general(projected, out_grad, (((0,), (0,)), ((),...  101 us
    psum x1, blocking collectives, per_device(): projected = lax.psum(partial_sum, 'tensor')  84.2 us
    all_gather x1, waiting for transfers between devices, per_device(): lax.all_gather(normalized, 'dp', axis=0, tiled=True)  42.9 us
    unnamed x8, local copies, waits for them, and re-layouts  30.8 us
    all_to_all x1, blocking collectives, sent_to_all(): return lax.all_to_all(copies, axis, split_axis=0, concat_axis=0, tiled=True)  11.2 us
    all_to_all x1, starting transfers between devices, sent_to_all(): return lax.all_to_all(copies, axis, split_axis=0, concat_axis=0, tiled=True)  9.45 us
    dot_general x1, matrix products, per_device(): lax.dot_general(projected, out_grad, (((0,), (0,)), ((), ())), preferred_...  9.15 us
    dot_general x1, matrix products, per_device(): jnp.dot(basis_rows, lax.all_gather(normalized, 'dp', axis=0, tiled=True),...  7.12 us
  transfers between devices with their start and end apart: 3, of which 2 were waited for; matrix products, arithmetic and copies ran while one was open for 8% of the time, Pallas kernels for 0%

commit v1 on v0

--- a/solution.py
+++ b/solution.py
@@ -35,7 +35,7 @@
     chosen = lax.dynamic_index_in_dim(split_cols, lax.axis_index("tensor"), 2, keepdims=False)
     chosen = chosen.reshape(token_rows, data_lanes * block_rows)
     partial_sum = jnp.dot(chosen, lane_blocks, preferred_element_type=jnp.float32)
-    projected = lax.psum(partial_sum, "tensor")
+    projected = jnp.sum(lax.all_gather(partial_sum, "tensor"), axis=0)
     projected = projected.astype(jnp.bfloat16)
     coefficients = lax.psum_scatter(
         lax.dot_general(

time: 321 us -> 563 us (1.75)
  waiting for transfers between devices: 144 us -> 464 us
  blocking collectives: 95.4 us -> 11 us
  other arithmetic: 2.16 us -> 10.3 us
    all_gather x0 -> x1, waiting for transfers between devices: none -> 327 us  [per_device(): projected = jnp.sum(lax.all_gather(partial_sum, 'tensor'), axis=0)]
    psum x1 -> x0, blocking collectives: 84.2 us -> none  [per_device(): projected = lax.psum(partial_sum, 'tensor')]
    reduce_sum x0 -> x1, other arithmetic: none -> 8.09 us  [per_device(): projected = jnp.sum(lax.all_gather(partial_sum, 'tensor'), axis=0)]
    reduce_scatter x1, waiting for transfers between devices: 101 us -> 94.4 us  [per_device(): lax.psum_scatter(lax.dot_general(projected, out_grad, (((0,), (0,)), ((),...]
  transfers between devices with their start and end apart: 3 -> 4, of which waited for: 2 -> 3; matrix products, arithmetic and copies ran while one was open for 8% -> 4% of each run, Pallas kernels for 0% -> 0%
where the time goes in v1:
time: 563 us; the launch traced here: 562 us
  waiting for transfers between devices  464 us (82%)
  local copies, waits for them, and re-layouts  34.6 us (6%)
  matrix products  18.9 us (3%)
  between operations  13.8 us (2%)
  blocking collectives  11 us (2%)
  other arithmetic  10.3 us (2%)
  starting transfers between devices  9.57 us (2%)
    all_gather x1, waiting for transfers between devices, per_device(): projected = jnp.sum(lax.all_gather(partial_sum, 'tensor'), axis=0)  327 us
    reduce_scatter x1, waiting for transfers between devices, per_device(): lax.psum_scatter(lax.dot_general(projected, out_grad, (((0,), (0,)), ((),...  94.4 us
    all_gather x1, waiting for transfers between devices, per_device(): lax.all_gather(normalized, 'dp', axis=0, tiled=True)  43 us
    unnamed x8, local copies, waits for them, and re-layouts  30.8 us
  transfers between devices with their start and end apart: 4, of which 3 were waited for; matrix products, arithmetic and copies ran while one was open for 4% of the time, Pallas kernels for 0%

profile of v1, /device:TPU:1, one launch (start us, length us, event | category | flops | bytes accessed | tf_op | source)
XLA Modules:
  0.0 562.0 jit_solution(8712035614415802570)
XLA Ops:
  7.2 1.9 broadcast_in_dim.6
  9.1 9.4 %all-to-all-start = ((bf16[16,64,512]{2,1,0:T(8,128)(2,1)}), bf16[16,64,512]{2,1,0:T(8,128)(2,1)S(1)}, u32[]{:S(2)}, u32[]{:S(2)}) async-start(bf16[16,64,512]{2,1,0:T(8,128)(2,1)} %broadcast_in_dim.6), calls=%async_computation | async-start | bytes 2097152 | tf_op jit(solution)/shard_map/all_to_all | solution.py:21
  18.5 0.0 all-gather.6.cloned.1.call-start
  18.6 22.4 %copy.9 = bf16[1024,8192]{0,1:T(8,128)(2,1)} copy(bf16[1024,8192]{1,0:T(8,128)(2,1)} %param.5) | data formatting | bytes 33554432 | tf_op args[0]
  41.0 1.9 constant_dynamic-slice_fusion
  42.8 0.0 all-to-all-done
  42.8 2.6 fusion.4
  45.4 0.0 all-gather.6.cloned.1.call-update
  45.5 0.0 reduce-scatter.2.cloned.1.call-start
  45.5 326.5 %all-gather.6.cloned.1.call-done = f32[8192,512]{1,0:T(8,128)} async-done(((f32[1024,512]{1,0:T(8,128)}), f32[8192,512]{1,0:T(8,128)}) %all-gather.6.cloned.1.call-update) | async-done | bytes 16777232 | tf_op jit(solution)/shard_map/all_gather | solution.py:38
  372.0 8.1 %reduce_sum.9 = bf16[1024,512]{1,0:T(8,128)(2,1)S(1)} reduce(f32[8,1024,512]{2,1,0:T(8,128)} %bitcast.14, f32[]{:T(128)} %constant.8.clone.1), dimensions={0}, to_apply=%region_0.1 | reduce | flops 3670016 | bytes 17825796 | tf_op jit(solution)/shard_map/reduce_sum | solution.py:38
  380.1 9.2 %fusion.5 = f32[512,3584]{1,0:T(8,128)} fusion(bf16[1024,512]{1,0:T(8,128)(2,1)S(1)} %reduce_sum.9, bf16[1024,3584]{1,0:T(8,128)(2,1)} %param.6), kind=kOutput, calls=%fused_computation.9 | convolution fusion | flops 3758096384 | bytes 15728640 | tf_op jit(solution)/shard_map/dot_general | solution.py:41
  389.3 0.0 copy-start
  389.3 0.0 copy-start.1
  389.3 0.0 copy-start.2
  389.3 0.0 reduce-scatter.2.cloned.1.call-update
  389.3 0.0 all-gather.4.cloned.1.call-start
  389.4 94.4 %reduce-scatter.2.cloned.1.call-done = f32[32,3584]{1,0:T(8,128)} async-done(((f32[512,3584]{1,0:T(8,128)}), f32[32,3584]{1,0:T(8,128)}) %reduce-scatter.2.cloned.1.call-update) | async-done | bytes 458768 | tf_op jit(solution)/shard_map/reduce_scatter | solution.py:40
  483.8 0.0 copy-done
  483.8 0.0 copy-done.1
  483.8 2.2 divide_convert_fusion
  485.9 0.0 all-gather.4.cloned.1.call-update
  485.9 0.0 copy-done.2
  486.0 11.0 %all_to_all.10 = bf16[8,64,512]{2,1,0:T(8,128)(2,1)S(1)} all-to-all(bf16[8,64,512]{2,1,0:T(8,128)(2,1)S(1)} %broadcast_in_dim.7), channel_id=1, replica_groups=mesh['dp'=16,'tensor'=8] {'tensor'}, dimensions={0} | all-to-all | bytes 1048576 | tf_op jit(solution)/shard_map/all_to_all | solution.py:21
  497.0 43.0 %all-gather.4.cloned.1.call-done = bf16[512,3584]{1,0:T(8,128)(2,1)} async-done(((bf16[32,3584]{1,0:T(8,128)(2,1)}), bf16[512,3584]{1,0:T(8,128)(2,1)}) %all-gather.4.cloned.1.call-update) | async-done | bytes 3670032 | tf_op jit(solution)/shard_map/all_gather | solution.py:56
  540.0 7.1 %convolution_bitcast_fusion = f32[512,3584]{0,1:T(8,128)} fusion(bf16[512,3584]{1,0:T(8,128)(2,1)} %all-gather.4.cloned.1.call-done, bf16[512,512]{1,0:T(8,128)(2,1)S(1)} %bitcast.15), kind=kOutput, calls=%fused_computation | convolution fusion | flops 1879048192 | bytes 11534336 | tf_op jit(solution)/shard_map/dot_general | solution.py:54
  547.1 8.4 %copy.10 = f32[512,3584]{1,0:T(8,128)} copy(f32[512,3584]{0,1:T(8,128)} %convolution_bitcast_fusion) | data formatting | bytes 14680064
  (1 shorter events, 0.0 us)
Async XLA Ops:
  9.1 33.8 %all-to-all-start = ((bf16[16,64,512]{2,1,0:T(8,128)(2,1)}), bf16[16,64,512]{2,1,0:T(8,128)(2,1)S(1)}, u32[]{:S(2)}, u32[]{:S(2)}) async-start(bf16[16,64,512]{2,1,0:T(8,128)(2,1)} %broadcast_in_dim.6), calls=%async_computation | async-start | bytes 2097152 | tf_op jit(solution)/shard_map/all_to_all | solution.py:21
  18.5 353.5 %all-gather.6.cloned.1.call-start = ((), (), s32[]{:S(2)}) async-start(), calls=%async_computation.5 | async-start | bytes 18874368 | tf_op jit(solution)/shard_map/all_gather | solution.py:38
  45.5 438.3 %reduce-scatter.2.cloned.1.call-start = ((), (), s32[]{:S(2)}) async-start(), calls=%async_computation.3 | async-start | bytes 7798784 | tf_op jit(solution)/shard_map/reduce_scatter | solution.py:40
  389.3 94.5 %copy-start = (f32[32,3584]{1,0:T(8,128)S(1)}, f32[32,3584]{1,0:T(8,128)}, u32[]{:S(2)}) copy-start(f32[32,3584]{1,0:T(8,128)} %param.8) | copy-start | bytes 1376260
  389.3 94.5 %copy-start.1 = (f32[32,3584]{1,0:T(8,128)S(1)}, f32[32,3584]{1,0:T(8,128)}, u32[]{:S(2)}) copy-start(f32[32,3584]{1,0:T(8,128)} %param.9) | copy-start | bytes 1376260
  389.3 96.7 %copy-start.2 = (bf16[64,512]{1,0:T(8,128)(2,1)S(1)}, bf16[64,512]{1,0:T(8,128)(2,1)}, u32[]{:S(2)}) copy-start(bf16[64,512]{1,0:T(8,128)(2,1)} %param.7) | copy-start | bytes 196612
  389.3 150.7 %all-gather.4.cloned.1.call-start = ((), (), s32[]{:S(2)}) async-start(), calls=%async_computation.4 | async-start | bytes 3899392 | tf_op jit(solution)/shard_map/all_gather | solution.py:56
Sparse Core Ops, SparseCore 0:
  45.6 326.3 all-gather.5
  389.4 94.2 reduce-scatter.1
  486.8 53.1 all-gather.3
